TPU v7x, 32 devices: a whole 2x2x4 slice. The times are simulated.
32 devices in a mesh: seq: 16 (over z, y, x), head: 2 (over core).
Axes of the slice: x: 2, y: 2, z: 4, core: 2. Of those that a mesh axis runs over, the one named last changes fastest.
Arguments:
- queries: bfloat16 [4096, 2048], P('seq', 'head'), may hold values from -6 to 6
- key_rows: bfloat16 [4096, 2048], P('seq', 'head'), may hold values from -6 to 6
- value_rows: bfloat16 [4096, 2048], P('seq', 'head'), may hold values from -6 to 6
- out_weight: bfloat16 [2048, 2048], P('head'), may hold values from -3 to 3
Outputs:
- layer_out: bfloat16 [4096, 2048], P('seq', 'head')
All inputs are finite; a program needn't handle non-finite values.
Results may differ from a plain program's by a relative error of at most 0.012.
Values may be sent and summed in bfloat16 or wider, within the bound.
A program may use at most 64 MiB of HBM per device.

v0:
```python
import jax
import jax.numpy as jnp
from jax import lax
from jax.sharding import PartitionSpec as P

HEAD_DIM = 128
LEAF = 256
LEVELS = 3


def from_partner(value, axis, bit):
    mask = 2**bit
    pairs = [(source, source ^ mask) for source in range(lax.axis_size(axis))]
    return lax.ppermute(value, axis, pairs)


def shifted(value, axis, by):
    count = lax.axis_size(axis)
    pairs = [(i, i + by) for i in range(count) if 0 <= i + by < count]
    return lax.ppermute(value, axis, pairs)


def averaged(matrix, factor):
    blocks = matrix.shape[0] // factor
    folded = matrix.astype(jnp.float32).reshape(blocks, factor, matrix.shape[1])
    return jnp.mean(folded, axis=1).astype(jnp.bfloat16)


def join_halves(own_part, peer_part, higher):
    return jnp.where(
        higher, jnp.concatenate([peer_part, own_part], 1), jnp.concatenate([own_part, peer_part], 1)
    )


def spread_sides(pieces, bit_count, device):
    for bit_index in range(bit_count):
        peer_part = from_partner(pieces, "seq", bit_index)
        higher = device // 2**bit_index % 2 == 1
        pieces = join_halves(pieces, peer_part, higher)
    return pieces


def level_terms(level_q, level_k, level_v, level_index, device, devices):
    row_count = level_q.shape[0]
    width_dh = level_q.shape[1]
    local_heads = width_dh // HEAD_DIM
    group_size = max(1, LEAF // row_count)
    bit_count = group_size.bit_length() - 1
    stacked = jnp.stack([level_k, level_v])
    if group_size > 1:
        first_block = device // group_size
        block_total = devices // group_size
    else:
        first_block = device * (row_count // LEAF)
        block_total = devices * (row_count // LEAF)
    from_lower = shifted(stacked, "seq", group_size)
    from_upper = shifted(stacked, "seq", -group_size)
    if group_size > 1:
        both_sides = spread_sides(jnp.concatenate([from_lower, from_upper], 0), bit_count, device)
        from_lower = both_sides[:2]
        from_upper = both_sides[2:]
    if group_size > 1:
        block_count = 1
        window = jnp.concatenate([from_lower[:, None], from_upper[:, None]], 2)
        query_blocks = level_q[None]
    else:
        block_count = row_count // LEAF
        extended = jnp.concatenate([from_lower, stacked, from_upper], 1)
        tiles = extended.reshape(2, block_count + 2, LEAF, width_dh)
        window = jnp.concatenate([tiles[:, :-2], tiles[:, 1:-1], tiles[:, 2:]], 2)
        query_blocks = level_q.reshape(block_count, LEAF, width_dh)
    query_rows = query_blocks.shape[1]
    global_block = first_block + jnp.arange(block_count, dtype=jnp.int32)
    lower_ok = jnp.broadcast_to((global_block > 0)[:, None], (block_count, LEAF))
    upper_ok = jnp.broadcast_to((global_block < block_total - 1)[:, None], (block_count, LEAF))
    if level_index == 0:
        usable = jnp.concatenate([lower_ok, jnp.ones((block_count, LEAF), bool), upper_ok], 1)
    else:
        usable = jnp.concatenate([lower_ok, upper_ok], 1)
    key_count = window.shape[2]
    query_heads = query_blocks.reshape(block_count, query_rows, local_heads, HEAD_DIM)
    key_heads = window[0].reshape(block_count, key_count, local_heads, HEAD_DIM)
    value_heads = window[1].reshape(block_count, key_count, local_heads, HEAD_DIM)
    scores = jnp.einsum(
        "bqhd,bkhd->bhqk", query_heads, key_heads, preferred_element_type=jnp.float32
    ) * HEAD_DIM ** (-0.5)
    scores = jnp.where(usable[:, None, None, :], scores, -jnp.inf)
    maxima = jnp.max(scores, axis=-1)
    weights = jnp.exp(scores - maxima[..., None]).astype(jnp.bfloat16)
    totals = jnp.sum(weights.astype(jnp.float32), axis=-1)
    numerator = jnp.einsum(
        "bhqk,bkhd->bqhd", weights, value_heads, preferred_element_type=jnp.float32
    )
    maxima = jnp.transpose(maxima, (0, 2, 1)).reshape(row_count, local_heads)
    totals = jnp.transpose(totals, (0, 2, 1)).reshape(row_count, local_heads)
    return (maxima, totals, numerator.reshape(row_count, local_heads, HEAD_DIM))


def body(queries, key_rows, value_rows, out_weight):
    device = lax.axis_index("seq")
    devices = lax.axis_size("seq")
    row_count = queries.shape[0]
    local_heads = queries.shape[1] // HEAD_DIM
    results = []
    for level_index in range(LEVELS + 1):
        factor = 2**level_index
        if level_index == 0:
            level_q, level_k, level_v = (queries, key_rows, value_rows)
        else:
            level_q = averaged(queries, factor)
            level_k = averaged(key_rows, factor)
            level_v = averaged(value_rows, factor)
        maxima, totals, numerator = level_terms(
            level_q, level_k, level_v, level_index, device, devices
        )
        results.append((factor, maxima, totals, numerator))
    row_max = results[0][1]
    for entry in results[1:]:
        factor, maxima = (entry[0], entry[1])
        spread = jnp.broadcast_to(
            maxima[:, None, :], (maxima.shape[0], factor, local_heads)
        ).reshape(row_count, local_heads)
        row_max = jnp.maximum(row_max, spread)
    denominator = jnp.zeros((row_count, local_heads), jnp.float32)
    numer_all = jnp.zeros((row_count, local_heads, HEAD_DIM), jnp.float32)
    for entry in results:
        factor, maxima, totals, numerator = entry
        blocks = maxima.shape[0]
        local_max = row_max.reshape(blocks, factor, local_heads)
        weight_level = factor * jnp.exp(maxima[:, None, :] - local_max)
        denominator = denominator + (weight_level * totals[:, None, :]).reshape(
            row_count, local_heads
        )
        numer_all = numer_all + (weight_level[..., None] * numerator[:, None, :, :]).reshape(
            row_count, local_heads, HEAD_DIM
        )
    attended = (
        (numer_all / denominator[..., None])
        .reshape(row_count, local_heads * HEAD_DIM)
        .astype(jnp.bfloat16)
    )
    partial_value = jnp.dot(attended, out_weight, preferred_element_type=jnp.float32)
    return lax.psum_scatter(
        partial_value.astype(jnp.bfloat16), "head", scatter_dimension=1, tiled=True
    )


def solution(mesh):
    in_specs = (P("seq", "head"), P("seq", "head"), P("seq", "head"), P("head", None))
    out_specs = P("seq", "head")
    return jax.shard_map(body, mesh=mesh, in_specs=in_specs, out_specs=out_specs, check_vma=False)
```

profile of v0, /device:TPU:1, one launch (start us, length us, event | category | flops | bytes accessed | tf_op | source)
XLA Modules:
  0.0 192.3 jit_solution(6171071696764907720)
XLA Ops:
  11.4 5.7 %collective-permute-start.9 = (bf16[2,32,1024]{2,1,0:T(8,128)(2,1)}, bf16[2,32,1024]{2,1,0:T(8,128)(2,1)}, u32[]{:S(2)}, u32[]{:S(2)}) collective-permute-start(bf16[2,32,1024]{2,1,0:T(8,128)(2,1)} %pad_maximum_fusion.8), channel_id=1, source_target_pairs={{0,16},{2,18},{4,20},{6,22},{8,24},{10,26},{12,28},{14,30},{1,17},... | collective-permute-start | bytes 393224 | tf_op jit(solution)/shard_map/ppermute | solution.py:20
  21.1 5.2 %collective-permute-start.5 = (bf16[2,64,1024]{2,1,0:T(8,128)(2,1)}, bf16[2,64,1024]{2,1,0:T(8,128)(2,1)}, u32[]{:S(2)}, u32[]{:S(2)}) collective-permute-start(bf16[2,64,1024]{2,1,0:T(8,128)(2,1)} %pad_maximum_fusion.7), channel_id=1, source_target_pairs={{0,8},{2,10},{4,12},{6,14},{8,16},{10,18},{12,20},{14,22},{16,24},... | collective-permute-start | bytes 786440 | tf_op jit(solution)/shard_map/ppermute | solution.py:20
  28.7 1.6 reshape.561
  30.9 2.5 %reduce_sum.120 = f32[128,1024]{1,0:T(8,128)S(1)} reduce(f32[128,2,1024]{2,1,0:T(2,128)} %reshape.561, f32[]{:T(128)} %constant.120.clone.1), dimensions={1}, to_apply=%region_2.3 | reduce | flops 131072 | bytes 1572868 | tf_op jit(solution)/shard_map/reduce_sum | solution.py:26
  33.4 2.1 %reduce_sum.121 = f32[128,1024]{1,0:T(8,128)} reduce(f32[128,2,1024]{2,1,0:T(2,128)S(1)} %reshape.562, f32[]{:T(128)} %constant.120.clone.1), dimensions={1}, to_apply=%region_3.4 | reduce | flops 131072 | bytes 1572868 | tf_op jit(solution)/shard_map/reduce_sum | solution.py:26
  39.5 5.0 %collective-permute-start = (bf16[2,256,1024]{2,1,0:T(8,128)(2,1)}, bf16[2,256,1024]{2,1,0:T(8,128)(2,1)}, u32[]{:S(2)}, u32[]{:S(2)}) collective-permute-start(bf16[2,256,1024]{2,1,0:T(8,128)(2,1)} %pad_maximum_fusion.5), channel_id=1, source_target_pairs={{0,2},{2,4},{4,6},{6,8},{8,10},{10,12},{12,14},{14,16},{16,18},{18... | collective-permute-start | bytes 3145736 | tf_op jit(solution)/shard_map/ppermute | solution.py:20
  46.0 3.1 %collective-permute-start.2 = (bf16[2,128,1024]{2,1,0:T(8,128)(2,1)}, bf16[2,128,1024]{2,1,0:T(8,128)(2,1)}, u32[]{:S(2)}, u32[]{:S(2)}) collective-permute-start(bf16[2,128,1024]{2,1,0:T(8,128)(2,1)} %pad_maximum_fusion.6), channel_id=1, source_target_pairs={{0,4},{2,6},{4,8},{6,10},{8,12},{10,14},{12,16},{14,18},{16,20},{1... | collective-permute-start | bytes 1572872 | tf_op jit(solution)/shard_map/ppermute | solution.py:20
  50.5 3.0 %collective-permute-start.11 = (bf16[4,32,1024]{2,1,0:T(8,128)(2,1)}, bf16[4,32,1024]{2,1,0:T(8,128)(2,1)}, u32[]{:S(2)}, u32[]{:S(2)}) collective-permute-start(bf16[4,32,1024]{2,1,0:T(8,128)(2,1)} %constant_dynamic-update-slice_fusion.4), channel_id=1, source_target_pairs={{0,2},{2,0},{4,6},{6,4},{8,10},{10,8},{12,14},{14,12},{16,18},{18,... | collective-permute-start | bytes 786440 | tf_op jit(solution)/shard_map/ppermute | solution.py:14
  57.5 2.3 %copy.86 = bf16[4,32,1024]{1,2,0:T(8,128)(2,1)} copy(bf16[4,32,1024]{2,1,0:T(8,128)(2,1)} %constant_dynamic-update-slice_fusion.4) | data formatting | bytes 524288 | tf_op jit(solution)/shard_map/concatenate | solution.py:59
  63.2 28.4 %collective-permute-done.11 = bf16[4,32,1024]{2,1,0:T(8,128)(2,1)} collective-permute-done((bf16[4,32,1024]{2,1,0:T(8,128)(2,1)}, bf16[4,32,1024]{2,1,0:T(8,128)(2,1)}, u32[]{:S(2)}, u32[]{:S(2)}) %collective-permute-start.11) | collective-permute-done | bytes 262176 | tf_op jit(solution)/shard_map/ppermute | solution.py:14
  91.6 2.3 %copy.85 = bf16[4,32,1024]{1,2,0:T(8,128)(2,1)} copy(bf16[4,32,1024]{2,1,0:T(8,128)(2,1)} %collective-permute-done.11) | data formatting | bytes 524288 | tf_op jit(solution)/shard_map/ppermute | solution.py:14
  93.9 3.5 %maximum_select_fusion.4 = bf16[4,64,1024]{1,2,0:T(8,128)(2,1)S(1)} fusion(bf16[4,32,1024]{1,2,0:T(8,128)(2,1)} %copy.86, bf16[4,32,1024]{1,2,0:T(8,128)(2,1)} %copy.85, pred[]{:T(512)S(6)} %eq.19), kind=kLoop, calls=%fused_computation.52 | loop fusion | flops 2359296 | bytes 1048577 | tf_op jit(solution)/shard_map/jit(_where)/select_n | solution.py:30
  98.8 1.9 %constant_dynamic-update-slice_fusion.1 = bf16[4,128,1024]{2,1,0:T(8,128)(2,1)} fusion(bf16[2,128,1024]{2,1,0:T(8,128)(2,1)} %collective-permute-done.2), kind=kLoop, calls=%fused_computation.90 | loop fusion | bytes 1048576
  100.8 1.9 constant_dynamic-update-slice_fusion
  104.1 2.6 %maximum_select_fusion.3 = bf16[4,128,1024]{2,1,0:T(8,128)(2,1)} fusion(bf16[4,64,1024]{2,1,0:T(8,128)(2,1)S(1)} %constant_dynamic-update-slice_fusion.2, bf16[4,64,1024]{2,1,0:T(8,128)(2,1)} %collective-permute-done.7, pred[]{:T(512)S(6)} %eq.19), kind=kLoop, calls=%fused_computation.51 | loop fusion | flops 4718592 | bytes 2097153 | tf_op jit(solution)/shard_map/jit(_where)/select_n | solution.py:30
  108.2 1.7 collective-permute-done.12
  109.9 2.4 %copy.90 = bf16[4,64,1024]{1,2,0:T(8,128)(2,1)} copy(bf16[4,64,1024]{2,1,0:T(8,128)(2,1)} %collective-permute-done.12) | data formatting | bytes 1048576 | tf_op jit(solution)/shard_map/ppermute | solution.py:14
  112.4 3.8 %maximum_select_fusion.5 = bf16[4,128,1024]{1,2,0:T(8,128)(2,1)} fusion(bf16[4,64,1024]{1,2,0:T(8,128)(2,1)S(1)} %maximum_select_fusion.4, bf16[4,64,1024]{1,2,0:T(8,128)(2,1)} %copy.90, pred[]{:T(512)S(6)} %eq.20), kind=kLoop, calls=%fused_computation.53 | loop fusion | flops 4718592 | bytes 2097153 | tf_op jit(solution)/shard_map/jit(_where)/select_n | solution.py:30
  116.3 1.8 pad_maximum_fusion
  118.9 2.0 %fusion.39 = (bf16[1,1,768,1024]{3,2,1,0:T(8,128)(2,1)}, bf16[1,1,768,1024]{3,2,1,0:T(8,128)(2,1)}) fusion(bf16[2,1,768,1024]{3,2,1,0:T(8,128)(2,1)S(1)} %pad_maximum_fusion.1), kind=kLoop, calls=%fused_computation.116 | loop fusion | bytes 6291456 | tf_op jit(solution)/shard_map/slice | solution.py:83
  120.9 1.7 copy.71
  122.6 4.1 %bitcast_reduce_fusion = (f32[8,256]{1,0:T(8,128)S(1)}, f32[8,768,256]{2,1,0:T(8,128)}) fusion(pred[768]{0:T(1024)(128)(4,1)S(1)} %fusion.28, bf16[768,8,128]{0,2,1:T(8,128)(2,1)S(1)} %bitcast.254, bf16[256,1024]{1,0:T(8,128)(2,1)S(1)} %copy-done.2), kind=kOutput, calls=%fused_computation.1 | convolution fusion | flops 407369728 | bytes 8397568 | tf_op jit(solution)/shard_map/bqhd,bkhd->bhqk/dot_general | solution.py:84
  126.8 1.7 copy.96
  128.5 4.3 %convert_reduce_fusion = (f32[8,256]{1,0:T(8,128)}, bf16[8,256,768]{1,2,0:T(8,128)(2,1)S(1)}) fusion(f32[8,256]{1,0:T(8,128)S(1)} %get-tuple-element.29, f32[8,768,256]{2,1,0:T(8,128)} %get-tuple-element.30, pred[768]{0:T(1024)(128)(4,1)S(1)} %fusion.28), kind=kLoop, calls=%fused_computation.4 | loop fusion | flops 9435136 | bytes 9454336 | tf_op jit(solution)/shard_map/reduce_sum | solution.py:90
  133.7 3.5 %maximum_select_fusion = bf16[4,256,1024]{2,1,0:T(8,128)(2,1)S(1)} fusion(bf16[4,128,1024]{2,1,0:T(8,128)(2,1)} %constant_dynamic-update-slice_fusion, bf16[4,128,1024]{2,1,0:T(8,128)(2,1)} %collective-permute-done.4, pred[]{:T(512)S(6)} %eq.19), kind=kLoop, calls=%fused_computation.9 | loop fusion | flops 9437184 | bytes 4194305 | tf_op jit(solution)/shard_map/jit(_where)/select_n | solution.py:30
  140.3 1.9 fusion.2
  143.7 2.1 %copy.106 = f32[128,8,128]{2,1,0:T(8,128)} copy(f32[128,8,128]{0,2,1:T(8,128)} %convolution_bitcast_fusion) | data formatting | bytes 1048576 | tf_op jit(solution)/shard_map/mul | solution.py:134
  148.0 3.3 %maximum_select_fusion.1 = bf16[4,256,1024]{2,1,0:T(8,128)(2,1)S(1)} fusion(bf16[4,128,1024]{2,1,0:T(8,128)(2,1)} %maximum_select_fusion.3, bf16[4,128,1024]{2,1,0:T(8,128)(2,1)} %collective-permute-done.8, pred[]{:T(512)S(6)} %eq.20), kind=kLoop, calls=%fused_computation.12 | loop fusion | flops 9437184 | bytes 4194305 | tf_op jit(solution)/shard_map/jit(_where)/select_n | solution.py:30
  155.5 1.6 fusion.42
  158.7 2.9 %maximum_select_fusion.2 = bf16[4,256,1024]{1,2,0:T(8,128)(2,1)S(1)} fusion(bf16[4,128,1024]{1,2,0:T(8,128)(2,1)} %maximum_select_fusion.5, bf16[4,128,1024]{1,2,0:T(8,128)(2,1)} %collective-permute-done.13, pred[]{:T(512)S(6)} %eq.21), kind=kLoop, calls=%fused_computation.15 | loop fusion | flops 9437184 | bytes 4194305 | tf_op jit(solution)/shard_map/jit(_where)/select_n | solution.py:30
  167.9 3.6 %convolution_convert_fusion = bf16[256,2048]{1,0:T(8,128)(2,1)} fusion(bf16[1024,2048]{1,0:T(8,128)(2,1)S(1)} %copy-done.3, f32[32,8,8,128]{3,2,1,0:T(8,128)S(1)} %bitcast.261, f32[32,8,8,128]{3,2,1,0:T(8,128)S(1)} %broadcast_bitcast_fusion, f32[32,8,8,128]{3,2,1,0:T(8,128)S(1)} %bitcast.260, f32[32,8,8,128]{3,2,1,0:T(8,128)S(1)} %bitcast.256, ...), kind=kOutput, calls=%fused_computation.8 | convolution fusion | flops 1076625408 | bytes 14680064 | tf_op jit(solution)/shard_map/dot_general | solution.py:142
  171.6 13.8 %reduce-scatter.2.cloned.1.call-done = bf16[256,1024]{1,0:T(8,128)(2,1)} async-done(((bf16[256,2048]{1,0:T(8,128)(2,1)}), bf16[256,1024]{1,0:T(8,128)(2,1)}) %reduce-scatter.2.cloned.1.call-update) | async-done | bytes 524304 | tf_op jit(solution)/shard_map/reduce_scatter | solution.py:143
  (156 shorter events, 50.7 us)
Async XLA Ops:
  6.5 10.5 %copy-start.1 = (bf16[256,1024]{1,0:T(8,128)(2,1)S(1)}, bf16[256,1024]{1,0:T(8,128)(2,1)}, u32[]{:S(2)}) copy-start(bf16[256,1024]{1,0:T(8,128)(2,1)} %param.5) | copy-start | bytes 1572868
  6.5 10.9 %copy-start = (bf16[256,1024]{1,0:T(8,128)(2,1)S(1)}, bf16[256,1024]{1,0:T(8,128)(2,1)}, u32[]{:S(2)}) copy-start(bf16[256,1024]{1,0:T(8,128)(2,1)} %param.6) | copy-start | bytes 1572868
  6.5 178.9 %reduce-scatter.2.cloned.1.call-start = ((), (), s32[]{:S(2)}) async-start(), calls=%async_computation.1 | async-start | bytes 1572864 | tf_op jit(solution)/shard_map/reduce_scatter | solution.py:143
  10.1 35.9 %collective-permute-start.10 = (bf16[2,32,1024]{2,1,0:T(8,128)(2,1)}, bf16[2,32,1024]{2,1,0:T(8,128)(2,1)S(1)}, u32[]{:S(2)}, u32[]{:S(2)}) collective-permute-start(bf16[2,32,1024]{2,1,0:T(8,128)(2,1)} %pad_maximum_fusion.8), channel_id=1, source_target_pairs={{16,0},{18,2},{20,4},{22,6},{24,8},{26,10},{28,12},{30,14},{17,1},... | collective-permute-start | bytes 393224 | tf_op jit(solution)/shard_map/ppermute | solution.py:20
  11.4 28.1 %collective-permute-start.9 = (bf16[2,32,1024]{2,1,0:T(8,128)(2,1)}, bf16[2,32,1024]{2,1,0:T(8,128)(2,1)}, u32[]{:S(2)}, u32[]{:S(2)}) collective-permute-start(bf16[2,32,1024]{2,1,0:T(8,128)(2,1)} %pad_maximum_fusion.8), channel_id=1, source_target_pairs={{0,16},{2,18},{4,20},{6,22},{8,24},{10,26},{12,28},{14,30},{1,17},... | collective-permute-start | bytes 393224 | tf_op jit(solution)/shard_map/ppermute | solution.py:20
  19.8 30.0 %collective-permute-start.6 = (bf16[2,64,1024]{2,1,0:T(8,128)(2,1)}, bf16[2,64,1024]{2,1,0:T(8,128)(2,1)S(1)}, u32[]{:S(2)}, u32[]{:S(2)}) collective-permute-start(bf16[2,64,1024]{2,1,0:T(8,128)(2,1)} %pad_maximum_fusion.7), channel_id=1, source_target_pairs={{8,0},{10,2},{12,4},{14,6},{16,8},{18,10},{20,12},{22,14},{24,16},... | collective-permute-start | bytes 786440 | tf_op jit(solution)/shard_map/ppermute | solution.py:20
  21.1 38.7 %collective-permute-start.5 = (bf16[2,64,1024]{2,1,0:T(8,128)(2,1)}, bf16[2,64,1024]{2,1,0:T(8,128)(2,1)}, u32[]{:S(2)}, u32[]{:S(2)}) collective-permute-start(bf16[2,64,1024]{2,1,0:T(8,128)(2,1)} %pad_maximum_fusion.7), channel_id=1, source_target_pairs={{0,8},{2,10},{4,12},{6,14},{8,16},{10,18},{12,20},{14,22},{16,24},... | collective-permute-start | bytes 786440 | tf_op jit(solution)/shard_map/ppermute | solution.py:20
  27.4 88.9 %collective-permute-start.1 = (bf16[2,256,1024]{2,1,0:T(8,128)(2,1)}, bf16[2,256,1024]{2,1,0:T(8,128)(2,1)}, u32[]{:S(2)}, u32[]{:S(2)}) collective-permute-start(bf16[2,256,1024]{2,1,0:T(8,128)(2,1)} %pad_maximum_fusion.5), channel_id=1, source_target_pairs={{2,0},{4,2},{6,4},{8,6},{10,8},{12,10},{14,12},{16,14},{18,16},{20... | collective-permute-start | bytes 3145736 | tf_op jit(solution)/shard_map/ppermute | solution.py:20
  33.4 4.1 %copy-start.2 = (bf16[256,1024]{1,0:T(8,128)(2,1)S(1)}, bf16[256,1024]{1,0:T(8,128)(2,1)}, u32[]{:S(2)}) copy-start(bf16[256,1024]{1,0:T(8,128)(2,1)} %param.4) | copy-start | bytes 1572868
  39.5 76.8 %collective-permute-start = (bf16[2,256,1024]{2,1,0:T(8,128)(2,1)}, bf16[2,256,1024]{2,1,0:T(8,128)(2,1)}, u32[]{:S(2)}, u32[]{:S(2)}) collective-permute-start(bf16[2,256,1024]{2,1,0:T(8,128)(2,1)} %pad_maximum_fusion.5), channel_id=1, source_target_pairs={{0,2},{2,4},{4,6},{6,8},{8,10},{10,12},{12,14},{14,16},{16,18},{18... | collective-permute-start | bytes 3145736 | tf_op jit(solution)/shard_map/ppermute | solution.py:20
  46.0 52.5 %collective-permute-start.2 = (bf16[2,128,1024]{2,1,0:T(8,128)(2,1)}, bf16[2,128,1024]{2,1,0:T(8,128)(2,1)}, u32[]{:S(2)}, u32[]{:S(2)}) collective-permute-start(bf16[2,128,1024]{2,1,0:T(8,128)(2,1)} %pad_maximum_fusion.6), channel_id=1, source_target_pairs={{0,4},{2,6},{4,8},{6,10},{8,12},{10,14},{12,16},{14,18},{16,20},{1... | collective-permute-start | bytes 1572872 | tf_op jit(solution)/shard_map/ppermute | solution.py:20
  49.8 0.7 copy-start.8
  50.5 41.1 %collective-permute-start.11 = (bf16[4,32,1024]{2,1,0:T(8,128)(2,1)}, bf16[4,32,1024]{2,1,0:T(8,128)(2,1)}, u32[]{:S(2)}, u32[]{:S(2)}) collective-permute-start(bf16[4,32,1024]{2,1,0:T(8,128)(2,1)} %constant_dynamic-update-slice_fusion.4), channel_id=1, source_target_pairs={{0,2},{2,0},{4,6},{6,4},{8,10},{10,8},{12,14},{14,12},{16,18},{18,... | collective-permute-start | bytes 786440 | tf_op jit(solution)/shard_map/ppermute | solution.py:14
  59.8 41.0 %collective-permute-start.3 = (bf16[2,128,1024]{2,1,0:T(8,128)(2,1)}, bf16[2,128,1024]{2,1,0:T(8,128)(2,1)}, u32[]{:S(2)}, u32[]{:S(2)}) collective-permute-start(bf16[2,128,1024]{2,1,0:T(8,128)(2,1)} %pad_maximum_fusion.6), channel_id=1, source_target_pairs={{4,0},{6,2},{8,4},{10,6},{12,8},{14,10},{16,12},{18,14},{20,16},{2... | collective-permute-start | bytes 1572872 | tf_op jit(solution)/shard_map/ppermute | solution.py:20
  91.6 12.5 %collective-permute-start.7 = (bf16[4,64,1024]{2,1,0:T(8,128)(2,1)S(1)}, bf16[4,64,1024]{2,1,0:T(8,128)(2,1)}, u32[]{:S(2)}, u32[]{:S(2)}) collective-permute-start(bf16[4,64,1024]{2,1,0:T(8,128)(2,1)S(1)} %constant_dynamic-update-slice_fusion.2), channel_id=1, source_target_pairs={{0,2},{2,0},{4,6},{6,4},{8,10},{10,8},{12,14},{14,12},{16,18},{18,... | collective-permute-start | bytes 1572872 | tf_op jit(solution)/shard_map/ppermute | solution.py:14
  98.5 11.4 %collective-permute-start.12 = (bf16[4,64,1024]{2,1,0:T(8,128)(2,1)}, bf16[4,64,1024]{2,1,0:T(8,128)(2,1)}, u32[]{:S(2)}, u32[]{:S(2)}) collective-permute-start(bf16[4,64,1024]{2,1,0:T(8,128)(2,1)} %copy.89), channel_id=1, source_target_pairs={{0,4},{2,6},{4,0},{6,2},{8,12},{10,14},{12,8},{14,10},{16,20},{18,... | collective-permute-start | bytes 1572872 | tf_op jit(solution)/shard_map/ppermute | solution.py:14
  102.6 31.1 %collective-permute-start.4 = (bf16[4,128,1024]{2,1,0:T(8,128)(2,1)}, bf16[4,128,1024]{2,1,0:T(8,128)(2,1)}, u32[]{:S(2)}, u32[]{:S(2)}) collective-permute-start(bf16[4,128,1024]{2,1,0:T(8,128)(2,1)} %constant_dynamic-update-slice_fusion), channel_id=1, source_target_pairs={{0,2},{2,0},{4,6},{6,4},{8,10},{10,8},{12,14},{14,12},{16,18},{18,... | collective-permute-start | bytes 3145736 | tf_op jit(solution)/shard_map/ppermute | solution.py:14
  106.7 41.2 %collective-permute-start.8 = (bf16[4,128,1024]{2,1,0:T(8,128)(2,1)}, bf16[4,128,1024]{2,1,0:T(8,128)(2,1)}, u32[]{:S(2)}, u32[]{:S(2)}) collective-permute-start(bf16[4,128,1024]{2,1,0:T(8,128)(2,1)} %maximum_select_fusion.3), channel_id=1, source_target_pairs={{0,4},{2,6},{4,0},{6,2},{8,12},{10,14},{12,8},{14,10},{16,20},{18,... | collective-permute-start | bytes 3145736 | tf_op jit(solution)/shard_map/ppermute | solution.py:14
  116.2 42.5 %collective-permute-start.13 = (bf16[4,128,1024]{1,2,0:T(8,128)(2,1)}, bf16[4,128,1024]{1,2,0:T(8,128)(2,1)}, u32[]{:S(2)}, u32[]{:S(2)}) collective-permute-start(bf16[4,128,1024]{1,2,0:T(8,128)(2,1)} %maximum_select_fusion.5), channel_id=1, source_target_pairs={{0,8},{2,10},{4,12},{6,14},{8,0},{10,2},{12,4},{14,6},{16,24},{18,... | collective-permute-start | bytes 3145736 | tf_op jit(solution)/shard_map/ppermute | solution.py:14
  137.6 2.7 %copy-start.5 = (bf16[128,1024]{0,1:T(8,128)(2,1)S(1)}, bf16[128,1024]{0,1:T(8,128)(2,1)}, u32[]{:S(2)}) copy-start(bf16[128,1024]{0,1:T(8,128)(2,1)} %copy.74) | copy-start | bytes 786436
  140.3 1.9 copy-start.6
  152.6 2.9 %copy-start.7 = (f32[64,1024]{1,0:T(8,128)S(1)}, f32[64,1024]{1,0:T(8,128)}, u32[]{:S(2)}) copy-start(f32[64,1024]{1,0:T(8,128)} %reduce_sum.122) | copy-start | bytes 786436
  152.6 2.9 %copy-start.13 = (pred[512]{0:T(512)(128)(4,1)S(1)}, pred[512]{0:T(512)(128)(4,1)}, u32[]{:S(2)}) copy-start(pred[512]{0:T(512)(128)(4,1)} %concatenate.80) | copy-start | bytes 1540
  161.7 0.7 copy-start.12
  163.0 1.5 copy-start.9
  163.0 1.5 copy-start.10
  163.0 1.5 copy-start.11
  163.5 1.7 copy-start.4
  165.7 2.2 %copy-start.3 = (bf16[1024,2048]{1,0:T(8,128)(2,1)S(1)}, bf16[1024,2048]{1,0:T(8,128)(2,1)}, u32[]{:S(2)}) copy-start(bf16[1024,2048]{1,0:T(8,128)(2,1)} %param.7) | copy-start | bytes 12582916
Sparse Core Ops, SparseCore 0:
  171.7 13.6 reduce-scatter.1
where the time goes:
time: 194 us; the launch traced here: 192 us
  other arithmetic  44.9 us (23%)
  local copies, waits for them, and re-layouts  44.2 us (23%)
  waiting for transfers between devices  44 us (23%)
  starting transfers between devices  30.3 us (16%)
  matrix products  14.6 us (8%)
  between operations  14.2 us (7%)
    ppermute x6, waiting for transfers between devices, from_partner(): return lax.ppermute(value, axis, pairs)  30.1 us
    ppermute x8, starting transfers between devices, shifted(): return lax.ppermute(value, axis, pairs)  24.3 us
    select_n x6, other arithmetic, join_halves(): jnp.where(higher, jnp.concatenate([peer_part, own_part], 1), jnp.concaten...  19.6 us
    reduce_scatter x1, waiting for transfers between devices, body(): lax.psum_scatter(partial_value.astype(jnp.bfloat16), 'head', scatter_dime...  13.8 us
    reduce_sum x9, other arithmetic, averaged(): return jnp.mean(folded, axis=1).astype(jnp.bfloat16)  11.6 us
    dot_general x4, matrix products, level_terms(): jnp.einsum('bqhd,bkhd->bhqk', query_heads, key_heads, preferred_element_t...  7.92 us
    unnamed x32, local copies, waits for them, and re-layouts  6.63 us
    slice x4, local copies, waits for them, and re-layouts, level_terms(): window[1].reshape(block_count, key_count, local_heads, HEAD_DIM)  6.58 us
  transfers between devices with their start and end apart: 15, of which 3 were waited for; matrix products, arithmetic and copies ran while one was open for 45% of the time, Pallas kernels for 0%

commit v1 on v0

v1 whole, which is shorter than its diff:
```python
import functools
import math

import jax
import jax.numpy as jnp
from jax import lax
from jax.experimental import pallas as pl
from jax.experimental.pallas import tpu as pltpu
from jax.sharding import PartitionSpec as P

HEAD_DIM = 128
LEAF = 256
LEVELS = 3
GROUP = 2 ** (LEVELS - 1)
MESH = pl.DeviceIdType.MESH
SCALE = HEAD_DIM ** (-0.5) * math.log2(math.e)
LOWEST = -1e30
F32 = jnp.float32
BF16 = jnp.bfloat16


def dot(a, b):
    return lax.dot_general(a, b, (((1,), (0,)), ((), ())), preferred_element_type=F32)


def dot_t(a, b):
    return lax.dot_general(a, b, (((1,), (1,)), ((), ())), preferred_element_type=F32)


def mean_matrix(rows):
    parts = []
    for level in range(1, LEVELS + 1):
        factor = 2**level
        r = lax.broadcasted_iota(jnp.int32, (rows // factor, rows), 0)
        c = lax.broadcasted_iota(jnp.int32, (rows // factor, rows), 1)
        parts.append(jnp.where(c // factor == r, 1.0 / factor, 0.0).astype(BF16))
    return parts


def order_of(i, rows):
    row = (i % (rows // 2**LEVELS)) * 2**LEVELS
    for bit in range(LEVELS):
        row = row + ((i // (rows // 2 ** (bit + 1))) % 2) * 2**bit
    return row


def attend(q, k, v, bias, before):
    s = dot_t(q, k)
    if bias is not None:
        s = s + bias
    top = jnp.max(s, axis=1, keepdims=True) * SCALE
    if before is not None:
        coarse_top, coarse_num = before
        top = jnp.maximum(top, coarse_top[:, :1])
    w = jnp.exp2(s * SCALE - top).astype(BF16)
    num = dot(w, jnp.concatenate([v, jnp.ones((v.shape[0], HEAD_DIM), BF16)], 1))
    if before is not None:
        a = 2.0 * jnp.exp2(coarse_top - top)
        num = num + jnp.concatenate([a, a], 1) * coarse_num
    return top, num


def twice(x, pieces):
    n = x.shape[0] // pieces
    out = []
    for i in range(pieces):
        out += [x[i * n : (i + 1) * n], x[i * n : (i + 1) * n]]
    return jnp.concatenate(out, 0)


def kernel(
    S, NH, q_ref, k_ref, v_ref, w_ref, o_ref,
    kv0, kv1, kv2, kv2own, kv3, c3, qp, q0, q1, q2, q3, n1, m1,
    attbuf, arecv, att, wv, psend, precv,
    s_kv, r_kv, s_q, r_q, s_l3, r_l3, s_z, r_z, s_a, r_a, s_p, r_p, s_w,
):
    rows, width = q_ref.shape
    G = GROUP
    w = width // G
    hg = w // HEAD_DIM
    NG = S // G
    s = lax.axis_index("seq")
    h = lax.axis_index("head")
    g = s // G
    p = s % G
    c = g // 2
    blocks3 = NG // 2
    has_lo, has_hi = g > 0, g < NG - 1
    has_lo3, has_hi3 = c > 0, c < blocks3 - 1
    r1, r2, r3 = rows // 2, rows // 4, rows // 8

    copy_w = pltpu.make_async_copy(w_ref, wv, s_w)
    copy_w.start()

    def cols(i):
        return pl.ds(pl.multiple_of(i * w, HEAD_DIM), w)

    def remote(src, dst, ss, rs, seq, head=None):
        ids = {"seq": seq} if head is None else {"head": head}
        return pltpu.make_async_remote_copy(
            src_ref=src, dst_ref=dst, send_sem=ss, recv_sem=rs, device_id=ids, device_id_type=MESH
        )

    barrier = pltpu.get_barrier_semaphore()
    for i in range(1, G):
        pl.semaphore_signal(barrier, 1, device_id={"seq": g * G + (p + i) % G}, device_id_type=MESH)
    for i in range(1, NH):
        pl.semaphore_signal(barrier, 1, device_id={"head": (h + i) % NH}, device_id_type=MESH)
    sibling = g + 1 - 2 * (g % 2)
    pl.semaphore_signal(barrier, 1, device_id={"seq": sibling * G + p}, device_id_type=MESH)
    for has, dc in ((has_lo3, -1), (has_hi3, 1)):
        @pl.when(has)
        def _():
            for u in range(2):
                for j in range(G):
                    pl.semaphore_signal(
                        barrier, 1, device_id={"seq": (2 * (c + dc) + u) * G + j}, device_id_type=MESH
                    )
    m1_, m2_, m3_ = mean_matrix(rows)
    c3[0] = dot(m3_, k_ref[...]).astype(BF16)
    c3[1] = dot(m3_, v_ref[...]).astype(BF16)
    sides = jnp.where(has_lo3, 1, 0) + jnp.where(has_hi3, 1, 0)
    pl.semaphore_wait(barrier, G - 1 + NH - 1 + 1 + 2 * G * sides)

    def l3_send(side, u, j):
        dc = (-1, 1)[side]
        slot = (2, 0)[side] + g % 2
        return remote(
            c3.at[:, :, cols(j)], kv3.at[:, slot, pl.ds(pl.multiple_of(p * r3, r3), r3)],
            s_l3.at[side, u, j], r_l3.at[slot, p], (2 * (c + dc) + u) * G + j,
        )

    def l3_recv(side, u, j):
        slot = 2 * side + u
        dc = (-1, 1)[side]
        return remote(
            c3.at[:, :, cols(j)], kv3.at[:, slot, pl.ds(j * r3, r3)],
            s_l3.at[side, u, j], r_l3.at[slot, j], (2 * (c + dc) + u) * G + j,
        )

    sides3 = ((0, has_lo3), (1, has_hi3))
    for side, has in sides3:
        @pl.when(has)
        def _():
            for j in range(G):
                for u in range(2):
                    l3_send(side, u, j).start()

    kv_refs = (k_ref, v_ref)

    def kv_send(i, t):
        d = (p + i) % G
        return remote(kv_refs[t].at[:, cols(d)], kv0.at[t, 1 + p], s_kv.at[t, i], r_kv.at[t, i], g * G + d)

    def kv_recv(i, t):
        d = (p + G - i) % G
        return remote(kv_refs[t].at[:, cols(d)], kv0.at[t, 1 + d], s_kv.at[t, i], r_kv.at[t, i], g * G + d)

    order = (2, 1, 3) if G == 4 else tuple(range(1, G))
    order = tuple(sorted(range(1, G), key=lambda i: order.index(i) if i in order else i))
    for t in range(2):
        for i in order:
            kv_send(i, t).start()

    i_ = lax.broadcasted_iota(jnp.int32, (rows, rows), 0)
    t_ = lax.broadcasted_iota(jnp.int32, (rows, rows), 1)
    perm = jnp.where(order_of(i_, rows) == t_, 1.0, 0.0).astype(BF16)
    qp[...] = dot(perm, q_ref[...]).astype(BF16)

    def q_send(i):
        d = (p + i) % G
        return remote(qp.at[:, cols(d)], q0.at[p], s_q.at[i], r_q.at[i], g * G + d)

    def q_recv(i):
        d = (p + G - i) % G
        return remote(qp.at[:, cols(d)], q0.at[d], s_q.at[i], r_q.at[i], g * G + d)

    for i in order:
        q_send(i).start()

    kv0[0, 1 + p] = k_ref[:, cols(p)]
    kv0[1, 1 + p] = v_ref[:, cols(p)]
    q0[p] = qp[:, cols(p)]

    for has, b0, b1, b2 in ((has_lo, 0, 0, 0), (has_hi, G + 1, 3, 1)):
        @pl.when(jnp.logical_not(has))
        def _():
            kv0[:, b0] = jnp.zeros((2, rows, w), BF16)
            kv1[:, b1] = jnp.zeros((2, LEAF, w), BF16)
            kv2[:, b2] = jnp.zeros((2, LEAF, w), BF16)
    for side, has in sides3:
        @pl.when(jnp.logical_not(has))
        def _():
            kv3[:, 2 * side : 2 * side + 2] = jnp.zeros((2, 2, LEAF // 2, w), BF16)

    for t in range(2):
        for i in order:
            kv_recv(i, t).wait_recv()

    def z_pair(dirn, kind):
        last = dirn == 0
        if kind == 0:
            src, dst = (kv0.at[:, G], kv0.at[:, 0]) if last else (kv0.at[:, 1], kv0.at[:, G + 1])
        elif kind == 1:
            a, b = (0, LEAF - r2) if last else (r2, LEAF - r2)
            src, dst = kv2own.at[:, pl.ds(a, b)], kv2.at[:, 0 if last else 1, pl.ds(a, b)]
        else:
            a, b = (0, LEAF - r1) if last else (r1, LEAF - r1)
            src = kv1.at[:, 2 if last else 1, pl.ds(a, b)]
            dst = kv1.at[:, 0 if last else 3, pl.ds(a, b)]
        to = s + G if last else s - G
        return remote(src, dst, s_z.at[dirn, kind], r_z.at[dirn, kind], to)

    dirs = ((0, has_hi), (1, has_lo))
    comes = ((0, has_lo), (1, has_hi))

    def z_start(kind):
        for dirn, has in dirs:
            @pl.when(has)
            def _():
                z_pair(dirn, kind).start()

    def z_wait(kind):
        for dirn, has in comes:
            @pl.when(has)
            def _():
                z_pair(dirn, kind).wait_recv()

    z_start(0)
    for j in range(G):
        for t in range(2):
            x = kv0[t, 1 + j]
            kv2own[t, j * r2 : (j + 1) * r2] = dot(m2_, x).astype(BF16)
    z_start(1)
    for j in range(G):
        for t in range(2):
            x = kv0[t, 1 + j]
            kv1[t, 1 + j // 2, (j % 2) * r1 : (j % 2 + 1) * r1] = dot(m1_, x).astype(BF16)
    z_start(2)

    for i in order:
        q_recv(i).wait_recv()
    for j in range(G):
        x = q0[j].astype(F32)
        x = x[:r1] + x[r1:]
        q1[j] = (x * 0.5).astype(BF16)
        x = x[:r2] + x[r2:]
        q2[j] = (x * 0.25).astype(BF16)
        x = x[:r3] + x[r3:]
        q3[j] = (x * 0.125).astype(BF16)

    def bias_of(keys, lo, hi):
        col = lax.broadcasted_iota(jnp.int32, (1, keys), 1)
        b_lo = jnp.where(lo, 0.0, LOWEST)
        b_hi = jnp.where(hi, 0.0, LOWEST)
        return jnp.where(col < LEAF, b_lo, jnp.where(col >= keys - LEAF, b_hi, 0.0))

    def wide(x):
        return jnp.broadcast_to(x, (x.shape[0], HEAD_DIM))

    for side, has in sides3:
        @pl.when(has)
        def _():
            for u in range(2):
                for j in range(G):
                    l3_recv(side, u, j).wait_recv()

    state = []
    for hh in range(hg):
        lanes = slice(hh * HEAD_DIM, (hh + 1) * HEAD_DIM)
        top, num = attend(
            q3[:, :, lanes].reshape(G * r3, HEAD_DIM),
            kv3[0, :, :, lanes].reshape(2 * LEAF, HEAD_DIM),
            kv3[1, :, :, lanes].reshape(2 * LEAF, HEAD_DIM),
            bias_of(2 * LEAF, has_lo3, has_hi3), None,
        )
        state.append((twice(wide(top), G), twice(num, G)))

    z_wait(0)
    for has, b0, b1, a1, b2, a2 in (
        (has_lo, 0, 0, LEAF - r1, 0, LEAF - r2), (has_hi, G + 1, 3, 0, 1, 0)
    ):
        @pl.when(has)
        def _():
            for t in range(2):
                x = kv0[t, b0]
                kv1[t, b1, a1 : a1 + r1] = dot(m1_, x).astype(BF16)
                kv2[t, b2, a2 : a2 + r2] = dot(m2_, x).astype(BF16)
    z_wait(1)
    for hh in range(hg):
        lanes = slice(hh * HEAD_DIM, (hh + 1) * HEAD_DIM)
        top, num = attend(
            q2[:, :, lanes].reshape(G * r2, HEAD_DIM),
            kv2[0, :, :, lanes].reshape(2 * LEAF, HEAD_DIM),
            kv2[1, :, :, lanes].reshape(2 * LEAF, HEAD_DIM),
            bias_of(2 * LEAF, has_lo, has_hi), state[hh],
        )
        state[hh] = (twice(wide(top), G), twice(num, G))
    z_wait(2)
    for hh in range(hg):
        lanes = slice(hh * HEAD_DIM, (hh + 1) * HEAD_DIM)
        for b in range(2):
            part = slice(b * LEAF, (b + 1) * LEAF)
            top, num = attend(
                q1[2 * b : 2 * b + 2, :, lanes].reshape(LEAF, HEAD_DIM),
                jnp.concatenate([kv1[0, b, :, lanes], kv1[0, b + 2, :, lanes]], 0),
                jnp.concatenate([kv1[1, b, :, lanes], kv1[1, b + 2, :, lanes]], 0),
                bias_of(2 * LEAF, has_lo if b == 0 else True, has_hi if b == 1 else True),
                (state[hh][0][part], state[hh][1][part]),
            )
            m1[hh, 2 * b : 2 * b + 2] = wide(top).reshape(2, r1, HEAD_DIM)
            n1[hh, 2 * b : 2 * b + 2] = num.reshape(2, r1, 2 * HEAD_DIM)

    def a_send(i, j):
        return remote(attbuf.at[j], arecv.at[p], s_a.at[i], r_a.at[i], g * G + j)

    def a_recv(i):
        d = (p + G - i) % G
        return remote(attbuf.at[d], arecv.at[d], s_a.at[i], r_a.at[i], g * G + d)

    def level0(step, carry):
        i = (step + 1) % G
        j = (p + i) % G
        bias = bias_of(3 * LEAF, jnp.logical_or(has_lo, j > 0), jnp.logical_or(has_hi, j < G - 1))
        for hh in range(hg):
            lanes = slice(hh * HEAD_DIM, (hh + 1) * HEAD_DIM)
            top, num = attend(
                q0[j, :, lanes],
                kv0[0, pl.ds(j, 3), :, lanes].reshape(3 * LEAF, HEAD_DIM),
                kv0[1, pl.ds(j, 3), :, lanes].reshape(3 * LEAF, HEAD_DIM),
                bias, (twice(m1[hh, j], 1), twice(n1[hh, j], 1)),
            )
            attbuf[j, :, lanes] = (num[:, :HEAD_DIM] / num[:, HEAD_DIM:]).astype(BF16)

        @pl.when(step < G - 1)
        def _():
            a_send(i, j).start()

        return carry

    lax.fori_loop(0, G, level0, 0)

    arecv[p] = attbuf[p]
    for i in range(1, G):
        a_recv(i).wait_recv()
    back = jnp.where(order_of(t_, rows) == i_, 1.0, 0.0).astype(BF16)
    for i in range(G):
        att[:, i * w : (i + 1) * w] = dot(back, arecv[i]).astype(BF16)

    copy_w.wait()
    cw = o_ref.shape[1]
    chunks = psend.shape[1]
    ch = cw // chunks

    def p_copy(i, n, peer):
        return remote(psend.at[i - 1, n], precv.at[i - 1, n], s_p.at[i - 1, n], r_p.at[i - 1, n], None, peer)

    for i in range(1, NH):
        t = (h + i) % NH
        for n in range(chunks):
            at = pl.multiple_of(t * cw + n * ch, HEAD_DIM)
            psend[i - 1, n] = dot(att[...], wv[:, pl.ds(at, ch)]).astype(BF16)
            p_copy(i, n, t).start()
    for n in range(chunks):
        at = pl.multiple_of(h * cw + n * ch, HEAD_DIM)
        total = dot(att[...], wv[:, pl.ds(at, ch)]).astype(BF16).astype(F32)
        for i in range(1, NH):
            p_copy(i, n, (h + NH - i) % NH).wait_recv()
            total = total + precv[i - 1, n].astype(F32)
        o_ref[:, n * ch : (n + 1) * ch] = total.astype(o_ref.dtype)

    for side, has in sides3:
        @pl.when(has)
        def _():
            for j in range(G):
                for u in range(2):
                    l3_send(side, u, j).wait_send()
    for i in order:
        for t in range(2):
            kv_send(i, t).wait_send()
        q_send(i).wait_send()
        a_send(i, (p + i) % G).wait_send()
    for kind in range(3):
        for dirn, has in dirs:
            @pl.when(has)
            def _():
                z_pair(dirn, kind).wait_send()
    for i in range(1, NH):
        for n in range(chunks):
            p_copy(i, n, (h + i) % NH).wait_send()


def solution(mesh):
    S, NH = mesh.shape["seq"], mesh.shape["head"]

    def body(queries, key_rows, value_rows, out_weight):
        rows, width = queries.shape
        full = out_weight.shape[1]
        G = GROUP
        w = width // G
        hg = w // HEAD_DIM
        assert rows == LEAF and S % (2 * G) == 0 and S >= 4 * G and w % HEAD_DIM == 0
        cw = full // NH
        chunks = 2
        vmem = pl.BlockSpec(memory_space=pltpu.VMEM)
        dma = pltpu.SemaphoreType.DMA
        V = pltpu.VMEM
        return pl.pallas_call(
            functools.partial(kernel, S, NH),
            out_shape=jax.ShapeDtypeStruct((rows, cw), queries.dtype),
            in_specs=[vmem, vmem, vmem, pl.BlockSpec(memory_space=pl.ANY)],
            out_specs=vmem,
            scratch_shapes=[
                V((2, G + 2, rows, w), BF16),
                V((2, 4, LEAF, w), BF16),
                V((2, 2, LEAF, w), BF16),
                V((2, LEAF, w), BF16),
                V((2, 4, LEAF // 2, w), BF16),
                V((2, rows // 8, width), BF16),
                V((rows, width), BF16),
                V((G, rows, w), BF16),
                V((G, rows // 2, w), BF16),
                V((G, rows // 4, w), BF16),
                V((G, rows // 8, w), BF16),
                V((hg, G, rows // 2, 2 * HEAD_DIM), F32),
                V((hg, G, rows // 2, HEAD_DIM), F32),
                V((G, rows, w), BF16),
                V((G, rows, w), BF16),
                V((rows, width), BF16),
                V((width, full), BF16),
                V((NH - 1, chunks, rows, cw // chunks), BF16),
                V((NH - 1, chunks, rows, cw // chunks), BF16),
                dma((2, G)), dma((2, G)),
                dma((G,)), dma((G,)),
                dma((2, 2, G)), dma((4, G)),
                dma((2, 3)), dma((2, 3)),
                dma((G,)), dma((G,)),
                dma((NH - 1, chunks)), dma((NH - 1, chunks)),
                dma,
            ],
            compiler_params=pltpu.CompilerParams(
                collective_id=0, has_side_effects=True, vmem_limit_bytes=56 * 2**20
            ),
        )(queries, key_rows, value_rows, out_weight)

    in_specs = (P("seq", "head"), P("seq", "head"), P("seq", "head"), P("head", None))
    return jax.shard_map(body, mesh=mesh, in_specs=in_specs, out_specs=P("seq", "head"), check_vma=False)
```

time: 194 us -> 52.1 us (0.27)
  Pallas kernels: 0 us -> 49.8 us
  other arithmetic: 44.9 us -> 0 us
  waiting for transfers between devices: 44 us -> 0 us
  local copies, waits for them, and re-layouts: 44.2 us -> 1.87 us
  starting transfers between devices: 30.3 us -> 0 us
  matrix products: 14.6 us -> 0 us
  between operations: 14.2 us -> 0.01 us
    pallas_call x0 -> x1, Pallas kernels: none -> 49.8 us  [body(): pl.pallas_call(functools.partial(kernel, S, NH), out_shape=jax.ShapeDtype...]
    ppermute x14 -> x0, starting transfers between devices: 30.3 us -> none  [the longest x8 24.3 us: shifted(): return lax.ppermute(value, axis, pairs)]
    ppermute x14 -> x0, waiting for transfers between devices: 30.1 us -> none  [the longest x6 30.1 us: from_partner(): return lax.ppermute(value, axis, pairs)]
    select_n x6 -> x0, other arithmetic: 19.6 us -> none  [join_halves(): jnp.where(higher, jnp.concatenate([peer_part, own_part], 1), jnp.concaten...]
    reduce_sum x13 -> x0, other arithmetic: 17.1 us -> none  [the longest x9 11.6 us: averaged(): return jnp.mean(folded, axis=1).astype(jnp.bfloat16)]
    dot_general x9 -> x0, matrix products: 14.6 us -> none  [the longest x4 7.92 us: level_terms(): jnp.einsum('bqhd,bkhd->bhqk', query_heads, key_heads, preferred_element_t...]
    reduce_scatter x1 -> x0, waiting for transfers between devices: 13.8 us -> none  [body(): lax.psum_scatter(partial_value.astype(jnp.bfloat16), 'head', scatter_dime...]
    slice x8 -> x0, local copies, waits for them, and re-layouts: 11.5 us -> none  [the longest x4 6.58 us: level_terms(): window[1].reshape(block_count, key_count, local_heads, HEAD_DIM)]
  transfers between devices with their start and end apart: 15 -> 0, of which waited for: 3 -> 0; matrix products, arithmetic and copies ran while one was open for 45% -> 0% of each run, Pallas kernels for 0% -> 0%
where the time goes in v1:
time: 52.1 us; the launch traced here: 51.7 us
  Pallas kernels  49.8 us (96%)
  local copies, waits for them, and re-layouts  1.87 us (4%)
    pallas_call x1, Pallas kernels, body(): pl.pallas_call(functools.partial(kernel, S, NH), out_shape=jax.ShapeDtype...  49.8 us
    unnamed x1, local copies, waits for them, and re-layouts  1.87 us

profile of v1, /device:TPU:1, one launch (start us, length us, event | category | flops | bytes accessed | tf_op | source)
XLA Modules:
  0.0 51.7 jit_solution(7842372340145764778)
XLA Ops:
  0.0 49.8 %shard_map.46 = bf16[256,1024]{1,0:T(8,128)(2,1)} custom-call(bf16[256,1024]{1,0:T(8,128)(2,1)} %q_ref.1, bf16[256,1024]{1,0:T(8,128)(2,1)} %k_ref.1, bf16[256,1024]{1,0:T(8,128)(2,1)} %v_ref.1, bf16[1024,2048]{1,0:T(8,128)(2,1)} %w_ref.1), custom_call_target="tpu_custom_call" | custom-call | tf_op jit(solution)/shard_map/pallas_call | solution.py:408
  49.8 1.9 %copy.6 = bf16[256,1024]{1,0:T(8,128)(2,1)} copy(bf16[256,1024]{1,0:T(8,128)(2,1)} %shard_map.46) | data formatting | bytes 1048576

commit v2 on v1

v2 whole, which is shorter than its diff:
```python
import functools
import math

import jax
import jax.numpy as jnp
from jax import lax
from jax.experimental import pallas as pl
from jax.experimental.pallas import tpu as pltpu
from jax.sharding import PartitionSpec as P

HEAD_DIM = 128
LEAF = 256
LEVELS = 3
GROUP = 2 ** (LEVELS - 1)
MESH = pl.DeviceIdType.MESH
SCALE = HEAD_DIM ** (-0.5) * math.log2(math.e)
LOWEST = -1e30
F32 = jnp.float32
BF16 = jnp.bfloat16
VMEM_BYTES = 56 * 2**20


def dot(a, b):
    return lax.dot_general(a, b, (((1,), (0,)), ((), ())), preferred_element_type=F32)


def dot_t(a, b):
    return lax.dot_general(a, b, (((1,), (1,)), ((), ())), preferred_element_type=F32)


def iota2(n, m):
    shape = (n, m)
    return lax.broadcasted_iota(jnp.int32, shape, 0), lax.broadcasted_iota(jnp.int32, shape, 1)


def mean_matrix(rows, level):
    r, c = iota2(rows >> level, rows)
    return jnp.where((c >> level) == r, 0.5**level, 0.0).astype(BF16)


def order_of(i, rows):
    top = rows.bit_length() - 1
    row = (i & (rows // 2**LEVELS - 1)) << LEVELS
    for bit in range(LEVELS):
        row = row | (((i >> (top - 1 - bit)) & 1) << bit)
    return row


def flip(p, i, bits):
    out = 0
    for b in range(bits):
        out = out + 2**b * ((p // 2**b + i // 2**b) % 2)
    return out


def attend(q, k, v, bias, before):
    s = dot_t(q, k)
    if bias is not None:
        s = s + bias
    top = jnp.max(s, axis=1, keepdims=True) * SCALE
    if before is not None:
        coarse_top, coarse_num = before
        top = jnp.maximum(top, coarse_top[:, :1])
    w = jnp.exp2(s * SCALE - top).astype(BF16)
    num = dot(w, jnp.concatenate([v, jnp.ones((v.shape[0], HEAD_DIM), BF16)], 1))
    if before is not None:
        a = 2.0 * jnp.exp2(coarse_top - top)
        num = num + jnp.concatenate([a, a], 1) * coarse_num
    return top, num


def twice(x, pieces):
    n = x.shape[0] // pieces
    out = []
    for i in range(pieces):
        out += [x[i * n : (i + 1) * n], x[i * n : (i + 1) * n]]
    return jnp.concatenate(out, 0)


def kernel(
    S, NH, q_hbm, k_hbm, v_hbm, w_hbm, o_ref,
    kv0, kv1, kv2, kv2own, kv3, c3, kvm, qm, qp, q0, q1, q2, q3, n1, m1,
    attbuf, arecv, att, wv, psend, precv,
    s_kv, r_kv, s_q, r_q, s_l3, r_l3, s_z, r_z, s_a, r_a, s_p, r_p, s_w, s_in, s_own,
):
    rows, width = q_hbm.shape
    G = GROUP
    D = HEAD_DIM
    w = width // G
    hg = w // D
    NG = S // G
    bits = G.bit_length() - 1
    s = lax.axis_index("seq")
    h = lax.axis_index("head")
    g = s // G
    p = s % G
    c = g // 2
    blocks3 = NG // 2
    has_lo, has_hi = g > 0, g < NG - 1
    has_lo3, has_hi3 = c > 0, c < blocks3 - 1
    sides3 = ((0, has_lo3), (1, has_hi3))
    r1, r2, r3 = rows // 2, rows // 4, rows // 8
    heads = range(hg)
    others = tuple(range(G - 1, 0, -1))

    barrier = pltpu.get_barrier_semaphore()
    for i in others:
        pl.semaphore_signal(barrier, 1, device_id={"seq": g * G + flip(p, i, bits)}, device_id_type=MESH)
    for i in range(1, NH):
        pl.semaphore_signal(barrier, 1, device_id={"head": (h + i) % NH}, device_id_type=MESH)
    sibling = g + 1 - 2 * (g % 2)
    pl.semaphore_signal(barrier, 1, device_id={"seq": sibling * G + p}, device_id_type=MESH)
    for has, dc in ((has_lo3, -1), (has_hi3, 1)):
        @pl.when(has)
        def _():
            for u in range(2):
                for j in range(G):
                    pl.semaphore_signal(
                        barrier, 1, device_id={"seq": (2 * (c + dc) + u) * G + j}, device_id_type=MESH
                    )

    kv_hbm = (k_hbm, v_hbm)
    loads = [pltpu.make_async_copy(kv_hbm[t], kvm.at[t], s_in.at[t]) for t in range(2)]
    loads.append(pltpu.make_async_copy(q_hbm, qm, s_in.at[2]))
    for load in (loads[2], loads[0], loads[1]):
        load.start()
    copy_w = pltpu.make_async_copy(w_hbm, wv, s_w)

    def lanes_of(i, hh):
        return pl.ds(pl.multiple_of((i * hg + hh) * D, D), D)

    def remote(src, dst, ss, rs, seq, head=None):
        ids = {"seq": seq} if head is None else {"head": head}
        return pltpu.make_async_remote_copy(
            src_ref=src, dst_ref=dst, send_sem=ss, recv_sem=rs, device_id=ids, device_id_type=MESH
        )

    own = []
    for hh in heads:
        for t in range(2):
            own.append(
                pltpu.make_async_copy(kv_hbm[t].at[:, lanes_of(p, hh)], kv0.at[hh, t, 1 + p], s_own.at[hh, t])
            )
            own[-1].start()

    sides = jnp.where(has_lo3, 1, 0) + jnp.where(has_hi3, 1, 0)
    pl.semaphore_wait(barrier, G - 1 + NH - 1 + 1 + 2 * G * sides)

    def kv_send(hh, t, i):
        d = flip(p, i, bits)
        return remote(
            kv_hbm[t].at[:, lanes_of(d, hh)], kv0.at[hh, t, 1 + p], s_kv.at[hh, t, i], r_kv.at[hh, t, i], g * G + d
        )

    def kv_recv(hh, t, i):
        d = flip(p, i, bits)
        return remote(
            kv_hbm[t].at[:, lanes_of(d, hh)], kv0.at[hh, t, 1 + d], s_kv.at[hh, t, i], r_kv.at[hh, t, i], g * G + d
        )

    for hh in heads:
        for t in range(2):
            for i in others:
                kv_send(hh, t, i).start()
    copy_w.start()

    def l3_send(side, u, j):
        dc = (-1, 1)[side]
        slot = (2, 0)[side] + g % 2
        lanes = slice(j * w, (j + 1) * w)
        return remote(
            c3.at[:, :, lanes], kv3.at[:, slot, pl.ds(pl.multiple_of(p * r3, r3), r3)],
            s_l3.at[side, u, j], r_l3.at[slot, p], (2 * (c + dc) + u) * G + j,
        )

    def l3_recv(side, u, j):
        slot = 2 * side + u
        dc = (-1, 1)[side]
        lanes = slice(j * w, (j + 1) * w)
        return remote(
            c3.at[:, :, lanes], kv3.at[:, slot, pl.ds(j * r3, r3)],
            s_l3.at[side, u, j], r_l3.at[slot, j], (2 * (c + dc) + u) * G + j,
        )

    loads[0].wait()
    loads[1].wait()
    m3_ = mean_matrix(rows, 3)
    for t in range(2):
        c3[t] = dot(m3_, kvm[t]).astype(BF16)
    for side, has in sides3:
        @pl.when(has)
        def _():
            for j in range(G):
                for u in range(2):
                    l3_send(side, u, j).start()

    loads[2].wait()
    i_, t_ = iota2(rows, rows)
    perm = jnp.where(order_of(i_, rows) == t_, 1.0, 0.0).astype(BF16)
    qp[...] = dot(perm, qm[...]).astype(BF16)

    def q_send(hh, i):
        d = flip(p, i, bits)
        return remote(qp.at[:, lanes_of(d, hh)], q0.at[hh, p], s_q.at[hh, i], r_q.at[hh, i], g * G + d)

    def q_recv(hh, i):
        d = flip(p, i, bits)
        return remote(qp.at[:, lanes_of(d, hh)], q0.at[hh, d], s_q.at[hh, i], r_q.at[hh, i], g * G + d)

    for hh in heads:
        for i in others:
            q_send(hh, i).start()
    for hh in heads:
        q0[hh, p] = qp[:, lanes_of(p, hh)]

    for has, b0, b1, b2 in ((has_lo, 0, 0, 0), (has_hi, G + 1, 3, 1)):
        @pl.when(jnp.logical_not(has))
        def _():
            kv0[:, :, b0] = jnp.zeros((hg, 2, rows, D), BF16)
            kv1[:, :, b1] = jnp.zeros((hg, 2, LEAF, D), BF16)
            kv2[:, :, b2] = jnp.zeros((hg, 2, LEAF, D), BF16)
    for side, has in sides3:
        @pl.when(jnp.logical_not(has))
        def _():
            kv3[:, 2 * side : 2 * side + 2] = jnp.zeros((2, 2, LEAF // 2, w), BF16)

    def z_pair(hh, dirn, kind):
        last = dirn == 0
        if kind == 0:
            src, dst = (
                (kv0.at[hh, :, G], kv0.at[hh, :, 0]) if last else (kv0.at[hh, :, 1], kv0.at[hh, :, G + 1])
            )
        elif kind == 1:
            a, b = (0, LEAF - r2) if last else (r2, LEAF - r2)
            src, dst = kv2own.at[hh, :, pl.ds(a, b)], kv2.at[hh, :, 0 if last else 1, pl.ds(a, b)]
        else:
            a, b = (0, LEAF - r1) if last else (r1, LEAF - r1)
            src = kv1.at[hh, :, 2 if last else 1, pl.ds(a, b)]
            dst = kv1.at[hh, :, 0 if last else 3, pl.ds(a, b)]
        to = s + G if last else s - G
        return remote(src, dst, s_z.at[hh, dirn, kind], r_z.at[hh, dirn, kind], to)

    dirs = ((0, has_hi), (1, has_lo))
    comes = ((0, has_lo), (1, has_hi))

    def z_start(hh, kind):
        for dirn, has in dirs:
            @pl.when(has)
            def _():
                z_pair(hh, dirn, kind).start()

    def z_wait(hh, kind):
        for dirn, has in comes:
            @pl.when(has)
            def _():
                z_pair(hh, dirn, kind).wait_recv()

    m1_ = mean_matrix(rows, 1)
    m2_ = mean_matrix(rows, 2)
    for copy in own:
        copy.wait()
    for hh in heads:
        for t in range(2):
            for i in others:
                kv_recv(hh, t, i).wait_recv()
        z_start(hh, 0)
        for t in range(2):
            for j in range(G):
                kv2own[hh, t, j * r2 : (j + 1) * r2] = dot(m2_, kv0[hh, t, 1 + j]).astype(BF16)
        z_start(hh, 1)
        for t in range(2):
            for j in range(G):
                at = (j % 2) * r1
                kv1[hh, t, 1 + j // 2, at : at + r1] = dot(m1_, kv0[hh, t, 1 + j]).astype(BF16)
        z_start(hh, 2)

    def bias_of(keys, lo, hi):
        col = lax.broadcasted_iota(jnp.int32, (1, keys), 1)
        b_lo = jnp.where(lo, 0.0, LOWEST)
        b_hi = jnp.where(hi, 0.0, LOWEST)
        return jnp.where(col < LEAF, b_lo, jnp.where(col >= keys - LEAF, b_hi, 0.0))

    def wide(x):
        return jnp.broadcast_to(x, (x.shape[0], D))

    for side, has in sides3:
        @pl.when(has)
        def _():
            for u in range(2):
                for j in range(G):
                    l3_recv(side, u, j).wait_recv()

    state = []
    for hh in heads:
        for i in others:
            q_recv(hh, i).wait_recv()
        for j in range(G):
            x = q0[hh, j].astype(F32)
            x = x[:r1] + x[r1:]
            q1[hh, j] = (x * 0.5).astype(BF16)
            x = x[:r2] + x[r2:]
            q2[hh, j] = (x * 0.25).astype(BF16)
            x = x[:r3] + x[r3:]
            q3[hh, j] = (x * 0.125).astype(BF16)
        lanes = slice(hh * D, (hh + 1) * D)
        top, num = attend(
            q3[hh].reshape(G * r3, D),
            kv3[0, :, :, lanes].reshape(2 * LEAF, D),
            kv3[1, :, :, lanes].reshape(2 * LEAF, D),
            bias_of(2 * LEAF, has_lo3, has_hi3), None,
        )
        state.append((twice(wide(top), G), twice(num, G)))

    for hh in heads:
        z_wait(hh, 0)
    for has, b0, b1, a1, b2, a2 in (
        (has_lo, 0, 0, LEAF - r1, 0, LEAF - r2), (has_hi, G + 1, 3, 0, 1, 0)
    ):
        @pl.when(has)
        def _():
            for hh in heads:
                for t in range(2):
                    x = kv0[hh, t, b0]
                    kv1[hh, t, b1, a1 : a1 + r1] = dot(m1_, x).astype(BF16)
                    kv2[hh, t, b2, a2 : a2 + r2] = dot(m2_, x).astype(BF16)
    for hh in heads:
        z_wait(hh, 1)
        top, num = attend(
            q2[hh].reshape(G * r2, D),
            kv2[hh, 0].reshape(2 * LEAF, D), kv2[hh, 1].reshape(2 * LEAF, D),
            bias_of(2 * LEAF, has_lo, has_hi), state[hh],
        )
        state[hh] = (twice(wide(top), G), twice(num, G))
    for hh in heads:
        z_wait(hh, 2)
        for b in range(2):
            part = slice(b * LEAF, (b + 1) * LEAF)
            top, num = attend(
                q1[hh, 2 * b : 2 * b + 2].reshape(LEAF, D),
                jnp.concatenate([kv1[hh, 0, b], kv1[hh, 0, b + 2]], 0),
                jnp.concatenate([kv1[hh, 1, b], kv1[hh, 1, b + 2]], 0),
                bias_of(2 * LEAF, has_lo if b == 0 else True, has_hi if b == 1 else True),
                (state[hh][0][part], state[hh][1][part]),
            )
            m1[hh, 2 * b : 2 * b + 2] = wide(top).reshape(2, r1, D)
            n1[hh, 2 * b : 2 * b + 2] = num.reshape(2, r1, 2 * D)

    def a_send(i):
        d = flip(p, i, bits)
        return remote(attbuf.at[d], arecv.at[p], s_a.at[i], r_a.at[i], g * G + d)

    def a_recv(i):
        d = flip(p, i, bits)
        return remote(attbuf.at[d], arecv.at[d], s_a.at[i], r_a.at[i], g * G + d)

    def level0(step, carry):
        i = G - 1 - step
        j = flip(p, i, bits)
        bias = bias_of(3 * LEAF, jnp.logical_or(has_lo, j > 0), jnp.logical_or(has_hi, j < G - 1))
        for hh in heads:
            top, num = attend(
                q0[hh, j],
                kv0[hh, 0, pl.ds(j, 3)].reshape(3 * LEAF, D),
                kv0[hh, 1, pl.ds(j, 3)].reshape(3 * LEAF, D),
                bias, (twice(m1[hh, j], 1), twice(n1[hh, j], 1)),
            )
            attbuf[j, :, hh * D : (hh + 1) * D] = (num[:, :D] / num[:, D:]).astype(BF16)

        @pl.when(step < G - 1)
        def _():
            a_send(i).start()

        return carry

    lax.fori_loop(0, G, level0, 0)

    back = jnp.where(order_of(t_, rows) == i_, 1.0, 0.0).astype(BF16)

    def place(d, x):
        att[:, pl.ds(pl.multiple_of(d * w, D), w)] = dot(back, x).astype(BF16)

    place(p, attbuf[p])
    for i in others:
        a_recv(i).wait_recv()
        d = flip(p, i, bits)
        place(d, arecv[d])

    copy_w.wait()
    cw = o_ref.shape[1]
    chunks = psend.shape[1]
    ch = cw // chunks

    def p_copy(i, n, peer):
        return remote(psend.at[i - 1, n], precv.at[i - 1, n], s_p.at[i - 1, n], r_p.at[i - 1, n], None, peer)

    for i in range(1, NH):
        t = (h + i) % NH
        for n in range(chunks):
            at = pl.multiple_of(t * cw + n * ch, D)
            psend[i - 1, n] = dot(att[...], wv[:, pl.ds(at, ch)]).astype(BF16)
            p_copy(i, n, t).start()
    for n in range(chunks):
        at = pl.multiple_of(h * cw + n * ch, D)
        total = dot(att[...], wv[:, pl.ds(at, ch)]).astype(BF16).astype(F32)
        for i in range(1, NH):
            p_copy(i, n, (h + NH - i) % NH).wait_recv()
            total = total + precv[i - 1, n].astype(F32)
        o_ref[:, n * ch : (n + 1) * ch] = total.astype(o_ref.dtype)

    for side, has in sides3:
        @pl.when(has)
        def _():
            for j in range(G):
                for u in range(2):
                    l3_send(side, u, j).wait_send()
    for i in others:
        for hh in heads:
            for t in range(2):
                kv_send(hh, t, i).wait_send()
            q_send(hh, i).wait_send()
        a_send(i).wait_send()
    for kind in range(3):
        for hh in heads:
            for dirn, has in dirs:
                @pl.when(has)
                def _():
                    z_pair(hh, dirn, kind).wait_send()
    for i in range(1, NH):
        for n in range(chunks):
            p_copy(i, n, (h + i) % NH).wait_send()


def solution(mesh):
    S, NH = mesh.shape["seq"], mesh.shape["head"]

    def body(queries, key_rows, value_rows, out_weight):
        rows, width = queries.shape
        full = out_weight.shape[1]
        G = GROUP
        D = HEAD_DIM
        w = width // G
        hg = w // D
        assert rows == LEAF and S % (2 * G) == 0 and S >= 4 * G and w % D == 0
        cw = full // NH
        chunks = 2
        dma = pltpu.SemaphoreType.DMA
        V = pltpu.VMEM
        return pl.pallas_call(
            functools.partial(kernel, S, NH),
            out_shape=jax.ShapeDtypeStruct((rows, cw), queries.dtype),
            in_specs=[pl.BlockSpec(memory_space=pl.ANY)] * 4,
            out_specs=pl.BlockSpec(memory_space=pltpu.VMEM),
            scratch_shapes=[
                V((hg, 2, G + 2, rows, D), BF16),
                V((hg, 2, 4, LEAF, D), BF16),
                V((hg, 2, 2, LEAF, D), BF16),
                V((hg, 2, LEAF, D), BF16),
                V((2, 4, LEAF // 2, w), BF16),
                V((2, rows // 8, width), BF16),
                V((2, rows, width), BF16),
                V((rows, width), BF16),
                V((rows, width), BF16),
                V((hg, G, rows, D), BF16),
                V((hg, G, rows // 2, D), BF16),
                V((hg, G, rows // 4, D), BF16),
                V((hg, G, rows // 8, D), BF16),
                V((hg, G, rows // 2, 2 * D), F32),
                V((hg, G, rows // 2, D), F32),
                V((G, rows, w), BF16),
                V((G, rows, w), BF16),
                V((rows, width), BF16),
                V((width, full), BF16),
                V((NH - 1, chunks, rows, cw // chunks), BF16),
                V((NH - 1, chunks, rows, cw // chunks), BF16),
                dma((hg, 2, G)), dma((hg, 2, G)),
                dma((hg, G)), dma((hg, G)),
                dma((2, 2, G)), dma((4, G)),
                dma((hg, 2, 3)), dma((hg, 2, 3)),
                dma((G,)), dma((G,)),
                dma((NH - 1, chunks)), dma((NH - 1, chunks)),
                dma, dma((3,)), dma((hg, 2)),
            ],
            compiler_params=pltpu.CompilerParams(
                collective_id=0, has_side_effects=True, vmem_limit_bytes=VMEM_BYTES
            ),
        )(queries, key_rows, value_rows, out_weight)

    in_specs = (P("seq", "head"), P("seq", "head"), P("seq", "head"), P("head", None))
    return jax.shard_map(body, mesh=mesh, in_specs=in_specs, out_specs=P("seq", "head"), check_vma=False)
```

time: 52.1 us -> 46.9 us (0.900)
  Pallas kernels: 49.8 us -> 44.9 us
    pallas_call x1, Pallas kernels: 49.8 us -> 44.9 us  [body(): pl.pallas_call(functools.partial(kernel, S, NH), out_shape=jax.ShapeDtype...]
where the time goes in v2:
time: 46.9 us; the launch traced here: 46.7 us
  Pallas kernels  44.9 us (96%)
  local copies, waits for them, and re-layouts  1.87 us (4%)
    pallas_call x1, Pallas kernels, body(): pl.pallas_call(functools.partial(kernel, S, NH), out_shape=jax.ShapeDtype...  44.9 us
    unnamed x1, local copies, waits for them, and re-layouts  1.87 us

profile of v2, /device:TPU:1, one launch (start us, length us, event | category | flops | bytes accessed | tf_op | source)
XLA Modules:
  0.0 46.7 jit_solution(17016700136946260803)
XLA Ops:
  0.0 44.9 %shard_map.46 = bf16[256,1024]{1,0:T(8,128)(2,1)} custom-call(bf16[256,1024]{1,0:T(8,128)(2,1)} %q_hbm.1, bf16[256,1024]{1,0:T(8,128)(2,1)} %k_hbm.1, bf16[256,1024]{1,0:T(8,128)(2,1)} %v_hbm.1, bf16[1024,2048]{1,0:T(8,128)(2,1)} %w_hbm.1), custom_call_target="tpu_custom_call" | custom-call | tf_op jit(solution)/shard_map/pallas_call | solution.py:448
  44.9 1.9 %copy.6 = bf16[256,1024]{1,0:T(8,128)(2,1)} copy(bf16[256,1024]{1,0:T(8,128)(2,1)} %shard_map.46) | data formatting | bytes 1048576

commit v3 on v2

--- a/solution.py
+++ b/solution.py
@@ -17,7 +17,7 @@
 LOWEST = -1e30
 F32 = jnp.float32
 BF16 = jnp.bfloat16
-VMEM_BYTES = 56 * 2**20
+VMEM_BYTES = 24 * 2**20
 
 
 def dot(a, b):
@@ -80,7 +80,7 @@
 def kernel(
     S, NH, q_hbm, k_hbm, v_hbm, w_hbm, o_ref,
     kv0, kv1, kv2, kv2own, kv3, c3, kvm, qm, qp, q0, q1, q2, q3, n1, m1,
-    attbuf, arecv, att, wv, psend, precv,
+    attbuf, arecv, att, acc, wv, psend, precv,
     s_kv, r_kv, s_q, r_q, s_l3, r_l3, s_z, r_z, s_a, r_a, s_p, r_p, s_w, s_in, s_own,
 ):
     rows, width = q_hbm.shape
@@ -290,7 +290,16 @@
                 for j in range(G):
                     l3_recv(side, u, j).wait_recv()
 
-    state = []
+    edges = ((has_lo, 0, 0, LEAF - r1, 0, LEAF - r2), (has_hi, G + 1, 3, 0, 1, 0))
+
+    def a_send(hh, i):
+        d = flip(p, i, bits)
+        return remote(attbuf.at[hh, d], arecv.at[hh, p], s_a.at[hh, i], r_a.at[hh, i], g * G + d)
+
+    def a_recv(hh, i):
+        d = flip(p, i, bits)
+        return remote(attbuf.at[hh, d], arecv.at[hh, d], s_a.at[hh, i], r_a.at[hh, i], g * G + d)
+
     for hh in heads:
         for i in others:
             q_recv(hh, i).wait_recv()
@@ -309,29 +318,22 @@
             kv3[1, :, :, lanes].reshape(2 * LEAF, D),
             bias_of(2 * LEAF, has_lo3, has_hi3), None,
         )
-        state.append((twice(wide(top), G), twice(num, G)))
-
-    for hh in heads:
+        state = (twice(wide(top), G), twice(num, G))
         z_wait(hh, 0)
-    for has, b0, b1, a1, b2, a2 in (
-        (has_lo, 0, 0, LEAF - r1, 0, LEAF - r2), (has_hi, G + 1, 3, 0, 1, 0)
-    ):
-        @pl.when(has)
-        def _():
-            for hh in heads:
+        for has, b0, b1, a1, b2, a2 in edges:
+            @pl.when(has)
+            def _():
                 for t in range(2):
                     x = kv0[hh, t, b0]
                     kv1[hh, t, b1, a1 : a1 + r1] = dot(m1_, x).astype(BF16)
                     kv2[hh, t, b2, a2 : a2 + r2] = dot(m2_, x).astype(BF16)
-    for hh in heads:
         z_wait(hh, 1)
         top, num = attend(
             q2[hh].reshape(G * r2, D),
             kv2[hh, 0].reshape(2 * LEAF, D), kv2[hh, 1].reshape(2 * LEAF, D),
-            bias_of(2 * LEAF, has_lo, has_hi), state[hh],
-        )
-        state[hh] = (twice(wide(top), G), twice(num, G))
-    for hh in heads:
+            bias_of(2 * LEAF, has_lo, has_hi), state,
+        )
+        state = (twice(wide(top), G), twice(num, G))
         z_wait(hh, 2)
         for b in range(2):
             part = slice(b * LEAF, (b + 1) * LEAF)
@@ -340,68 +342,55 @@
                 jnp.concatenate([kv1[hh, 0, b], kv1[hh, 0, b + 2]], 0),
                 jnp.concatenate([kv1[hh, 1, b], kv1[hh, 1, b + 2]], 0),
                 bias_of(2 * LEAF, has_lo if b == 0 else True, has_hi if b == 1 else True),
-                (state[hh][0][part], state[hh][1][part]),
+                (state[0][part], state[1][part]),
             )
             m1[hh, 2 * b : 2 * b + 2] = wide(top).reshape(2, r1, D)
             n1[hh, 2 * b : 2 * b + 2] = num.reshape(2, r1, 2 * D)
-
-    def a_send(i):
-        d = flip(p, i, bits)
-        return remote(attbuf.at[d], arecv.at[p], s_a.at[i], r_a.at[i], g * G + d)
-
-    def a_recv(i):
-        d = flip(p, i, bits)
-        return remote(attbuf.at[d], arecv.at[d], s_a.at[i], r_a.at[i], g * G + d)
-
-    def level0(step, carry):
-        i = G - 1 - step
-        j = flip(p, i, bits)
-        bias = bias_of(3 * LEAF, jnp.logical_or(has_lo, j > 0), jnp.logical_or(has_hi, j < G - 1))
-        for hh in heads:
+        for i in others + (0,):
+            j = flip(p, i, bits)
+            bias = bias_of(3 * LEAF, jnp.logical_or(has_lo, j > 0), jnp.logical_or(has_hi, j < G - 1))
             top, num = attend(
                 q0[hh, j],
                 kv0[hh, 0, pl.ds(j, 3)].reshape(3 * LEAF, D),
                 kv0[hh, 1, pl.ds(j, 3)].reshape(3 * LEAF, D),
                 bias, (twice(m1[hh, j], 1), twice(n1[hh, j], 1)),
             )
-            attbuf[j, :, hh * D : (hh + 1) * D] = (num[:, :D] / num[:, D:]).astype(BF16)
-
-        @pl.when(step < G - 1)
-        def _():
-            a_send(i).start()
-
-        return carry
-
-    lax.fori_loop(0, G, level0, 0)
+            attbuf[hh, j] = (num[:, :D] / num[:, D:]).astype(BF16)
+            if i:
+                a_send(hh, i).start()
 
     back = jnp.where(order_of(t_, rows) == i_, 1.0, 0.0).astype(BF16)
-
-    def place(d, x):
-        att[:, pl.ds(pl.multiple_of(d * w, D), w)] = dot(back, x).astype(BF16)
-
-    place(p, attbuf[p])
-    for i in others:
-        a_recv(i).wait_recv()
-        d = flip(p, i, bits)
-        place(d, arecv[d])
-
-    copy_w.wait()
     cw = o_ref.shape[1]
     chunks = psend.shape[1]
     ch = cw // chunks
+    copy_w.wait()
+
+    def project(hh, at):
+        lanes = pl.ds(at if isinstance(at, int) else pl.multiple_of(at, D), ch)
+        weight = jnp.concatenate([wv[(d * hg + hh) * D : (d * hg + hh + 1) * D, lanes] for d in range(G)], 0)
+        out = dot(att[hh], weight)
+        return out if hh == 0 else out + acc[:, lanes]
 
     def p_copy(i, n, peer):
         return remote(psend.at[i - 1, n], precv.at[i - 1, n], s_p.at[i - 1, n], r_p.at[i - 1, n], None, peer)
 
+    for hh in heads:
+        arecv[hh, p] = attbuf[hh, p]
+        for i in others:
+            a_recv(hh, i).wait_recv()
+        for d in range(G):
+            att[hh, :, d * D : (d + 1) * D] = dot(back, arecv[hh, d]).astype(BF16)
+        if hh < hg - 1:
+            for n in range(NH * chunks):
+                acc[:, n * ch : (n + 1) * ch] = project(hh, n * ch)
+    last = hg - 1
     for i in range(1, NH):
         t = (h + i) % NH
         for n in range(chunks):
-            at = pl.multiple_of(t * cw + n * ch, D)
-            psend[i - 1, n] = dot(att[...], wv[:, pl.ds(at, ch)]).astype(BF16)
+            psend[i - 1, n] = project(last, t * cw + n * ch).astype(BF16)
             p_copy(i, n, t).start()
     for n in range(chunks):
-        at = pl.multiple_of(h * cw + n * ch, D)
-        total = dot(att[...], wv[:, pl.ds(at, ch)]).astype(BF16).astype(F32)
+        total = project(last, h * cw + n * ch).astype(BF16).astype(F32)
         for i in range(1, NH):
             p_copy(i, n, (h + NH - i) % NH).wait_recv()
             total = total + precv[i - 1, n].astype(F32)
@@ -418,7 +407,7 @@
             for t in range(2):
                 kv_send(hh, t, i).wait_send()
             q_send(hh, i).wait_send()
-        a_send(i).wait_send()
+            a_send(hh, i).wait_send()
     for kind in range(3):
         for hh in heads:
             for dirn, has in dirs:
@@ -448,7 +437,7 @@
         return pl.pallas_call(
             functools.partial(kernel, S, NH),
             out_shape=jax.ShapeDtypeStruct((rows, cw), queries.dtype),
-            in_specs=[pl.BlockSpec(memory_space=pl.ANY)] * 4,
+            in_specs=[pl.BlockSpec(memory_space=pltpu.HBM)] * 4,
             out_specs=pl.BlockSpec(memory_space=pltpu.VMEM),
             scratch_shapes=[
                 V((hg, 2, G + 2, rows, D), BF16),
@@ -466,9 +455,10 @@
                 V((hg, G, rows // 8, D), BF16),
                 V((hg, G, rows // 2, 2 * D), F32),
                 V((hg, G, rows // 2, D), F32),
-                V((G, rows, w), BF16),
-                V((G, rows, w), BF16),
-                V((rows, width), BF16),
+                V((hg, G, rows, D), BF16),
+                V((hg, G, rows, D), BF16),
+                V((hg, rows, G * D), BF16),
+                V((rows, full), F32),
                 V((width, full), BF16),
                 V((NH - 1, chunks, rows, cw // chunks), BF16),
                 V((NH - 1, chunks, rows, cw // chunks), BF16),
@@ -476,14 +466,14 @@
                 dma((hg, G)), dma((hg, G)),
                 dma((2, 2, G)), dma((4, G)),
                 dma((hg, 2, 3)), dma((hg, 2, 3)),
-                dma((G,)), dma((G,)),
+                dma((hg, G)), dma((hg, G)),
                 dma((NH - 1, chunks)), dma((NH - 1, chunks)),
                 dma, dma((3,)), dma((hg, 2)),
             ],
             compiler_params=pltpu.CompilerParams(
                 collective_id=0, has_side_effects=True, vmem_limit_bytes=VMEM_BYTES
             ),
-        )(queries, key_rows, value_rows, out_weight)
+        )(*[pltpu.with_memory_space_constraint(x, pltpu.HBM) for x in (queries, key_rows, value_rows, out_weight)])
 
     in_specs = (P("seq", "head"), P("seq", "head"), P("seq", "head"), P("head", None))
     return jax.shard_map(body, mesh=mesh, in_specs=in_specs, out_specs=P("seq", "head"), check_vma=False)

time: 46.9 us -> 43.4 us (0.925)
  Pallas kernels: 44.9 us -> 42.5 us
  local copies, waits for them, and re-layouts: 1.87 us -> 0.8 us
    pallas_call x1, Pallas kernels: 44.9 us -> 42.5 us  [body(): pl.pallas_call(functools.partial(kernel, S, NH), out_shape=jax.ShapeDtype...]
    unnamed x1, local copies, waits for them, and re-layouts: 1.87 us -> 0.8 us
where the time goes in v3:
time: 43.4 us; the launch traced here: 43.3 us
  Pallas kernels  42.5 us (98%)
  local copies, waits for them, and re-layouts  0.8 us (2%)
    pallas_call x1, Pallas kernels, body(): pl.pallas_call(functools.partial(kernel, S, NH), out_shape=jax.ShapeDtype...  42.5 us

profile of v3, /device:TPU:1, one launch (start us, length us, event | category | flops | bytes accessed | tf_op | source)
XLA Modules:
  0.0 43.3 jit_solution(9738370924612934826)
XLA Ops:
  0.0 42.5 %shard_map.46 = bf16[256,1024]{1,0:T(8,128)(2,1)S(1)} custom-call(bf16[256,1024]{1,0:T(8,128)(2,1)} %q_hbm.1, bf16[256,1024]{1,0:T(8,128)(2,1)} %k_hbm.1, bf16[256,1024]{1,0:T(8,128)(2,1)} %v_hbm.1, bf16[1024,2048]{1,0:T(8,128)(2,1)} %w_hbm.1), custom_call_target="tpu_custom_call" | custom-call | tf_op jit(solution)/shard_map/pallas_call | solution.py:437
  42.5 0.8 %copy.6 = bf16[256,1024]{1,0:T(8,128)(2,1)} copy(bf16[256,1024]{1,0:T(8,128)(2,1)S(1)} %shard_map.46) | data formatting | bytes 1048576
